TPU v7x, 32 devices: a whole 2x2x4 slice. The times are simulated.
32 devices in a mesh: dp: 8 (over y, x, core), seq: 4 (over z).
Axes of the slice: x: 2, y: 2, z: 4, core: 2. Of those that a mesh axis runs over, the one named last changes fastest.
Arguments:
- block_input: bfloat16 [24, 1024, 1024], P('dp', 'seq'), may hold values from -6 to 6
- seg_start: int32 [24, 1024], P('dp'), may hold values from 0 to 1023, as said below
- ln1_gain: float32 [1024], replicated, may hold values from 0.5 to 1.5
- ln1_bias: float32 [1024], replicated, may hold values from -1.75 to 1.75
- qkv_weight: bfloat16 [1024, 3072], P('dp'), may hold values from -0.1875 to 0.1875
- query_bias: float32 [1024], replicated, may hold values from -1.75 to 1.75
- value_bias: float32 [1024], replicated, may hold values from -1.75 to 1.75
- query_adapter_reduce: bfloat16 [1024, 4], replicated, may hold values from -0.1875 to 0.1875
- query_up: bfloat16 [4, 1024], replicated, may hold values from -0.1875 to 0.1875
- value_adapter_reduce: bfloat16 [1024, 4], replicated, may hold values from -0.1875 to 0.1875
- value_up: bfloat16 [4, 1024], replicated, may hold values from -0.1875 to 0.1875
- out_weight: bfloat16 [1024, 1024], P('dp'), may hold values from -0.75 to 0.75
- out_bias: float32 [1024], replicated, may hold values from -1.75 to 1.75
- ln2_gain: float32 [1024], replicated, may hold values from 0.5 to 1.5
- ln2_bias: float32 [1024], replicated, may hold values from -1.75 to 1.75
- fc_weight: bfloat16 [1024, 4096], P('dp'), may hold values from -0.1875 to 0.1875
- fc_bias: float32 [4096], replicated, may hold values from -1.75 to 1.75
- proj_weight: bfloat16 [4096, 1024], P('dp'), may hold values from -0.09375 to 0.09375
- proj_bias: float32 [1024], replicated, may hold values from -1.75 to 1.75
- grad_out: bfloat16 [24, 1024, 1024], P('dp', 'seq'), may hold values from -6 to 6
Outputs:
- block_output: bfloat16 [24, 1024, 1024], P('dp', 'seq')
- grad_input: float32 [24, 1024, 1024], P('dp', 'seq')
- grad_query_down: float32 [1024, 4], replicated
- grad_query_up: float32 [4, 1024], replicated
- grad_value_down: float32 [1024, 4], replicated
- grad_value_up: float32 [4, 1024], replicated
Inputs may be any that keep to these rules, and one draw needn't show every extreme that they name: `seg_start`: each entry is the first position of its token's document within the row: it is at most the token's own position, position 0 has 0, and equal entries form runs of consecutive tokens whose start is the entry itself. The last position of every row starts its own document. In every row one document begins within the row's first 1 / N of positions and ends within its last 1 / N, N being the number of devices along seq.
All inputs are finite; a program needn't handle non-finite values.
Results may differ from a plain program's by a relative error of at most 0.014.
Values may be sent and summed in bfloat16 or wider, within the bound.
A program may use at most 192 MiB of HBM per device.

v0:
```python
from functools import partial
import jax
import jax.numpy as jnp
from jax import lax
from jax.sharding import PartitionSpec as P

HEAD = 64
NORM_EPSILON = 1e-05
ADAPTER_SCALE = 8.0
MASKED = -1e30


def for_sending(value):

    def short(part):
        return part.astype(jnp.bfloat16) if part.dtype == jnp.float32 else part

    return jax.tree.map(short, value)


def norm_forward(row_values, norm_gain, norm_shift):
    average = jnp.mean(row_values, axis=-1, keepdims=True)
    centered = row_values - average
    inverse = lax.rsqrt(jnp.mean(centered * centered, axis=-1, keepdims=True) + NORM_EPSILON)
    normed = centered * inverse
    return (normed * norm_gain + norm_shift, normed, inverse)


def norm_backward(gradient, normed, inverse, norm_gain):
    scaled = gradient * norm_gain
    return inverse * (
        scaled
        - jnp.mean(scaled, axis=-1, keepdims=True)
        - normed * jnp.mean(scaled * normed, axis=-1, keepdims=True)
    )


def fold_with(left_side, total_sum, weight_piece):
    columns = lax.slice_in_dim(left_side, 0, weight_piece.shape[0], axis=1)
    return total_sum + jnp.dot(columns, weight_piece, preferred_element_type=jnp.float32)


def times_transposed(left_side, right_side):
    return lax.dot_general(
        left_side, right_side, (((1,), (1,)), ((), ())), preferred_element_type=jnp.float32
    )


def across_token_rows(left_side, right_side):
    return lax.dot_general(
        left_side, right_side, (((0,), (0,)), ((), ())), preferred_element_type=jnp.float32
    )


def map_with(left_side, weight_piece):
    return times_transposed(left_side, weight_piece)


def mask_for(document_starts, offset, block_rows, length):
    query_pos = offset + jnp.arange(block_rows, dtype=jnp.int32)
    key_pos = jnp.arange(length, dtype=jnp.int32)
    query_start = document_starts[offset : offset + block_rows]
    return (key_pos[None, :] <= query_pos[:, None]) & (key_pos[None, :] >= query_start[:, None])


def split_heads(head_layout):
    length = head_layout.shape[0]
    head_count = head_layout.shape[2] // HEAD
    return (
        head_layout[:, 0].reshape(length, head_count, HEAD),
        head_layout[:, 1].reshape(length, head_count, HEAD),
        head_layout[:, 2].reshape(length, head_count, HEAD),
    )


def attend_row(row_entry):
    head_layout, document_starts = row_entry
    query_heads, key_heads, value_heads = split_heads(head_layout)
    length = head_layout.shape[0]
    block_rows = min(512, length)
    score_scale = HEAD ** (-0.5)
    mixed_parts = []
    total_parts = []
    for offset in range(0, length, block_rows):
        allowed = mask_for(document_starts, offset, block_rows, length)
        scores = (
            jnp.einsum(
                "qhd,khd->hqk",
                query_heads[offset : offset + block_rows],
                key_heads,
                preferred_element_type=jnp.float32,
            )
            * score_scale
        )
        scores = jnp.where(allowed[None], scores, MASKED)
        highest = jnp.max(scores, axis=-1, keepdims=True)
        weights = jnp.exp(scores - highest)
        denominator = jnp.sum(weights, axis=-1, keepdims=True)
        probabilities = (weights / denominator).astype(jnp.bfloat16)
        mixed_rows = jnp.einsum(
            "hqk,khd->qhd", probabilities, value_heads, preferred_element_type=jnp.float32
        )
        mixed_parts.append(mixed_rows.reshape(block_rows, -1))
        total_parts.append((highest + jnp.log(denominator))[:, :, 0])
    return (jnp.concatenate(mixed_parts, 0).astype(jnp.bfloat16), jnp.concatenate(total_parts, 1))


def attend_back(row_entry):
    head_layout, grad_mixed, log_total, document_starts = row_entry
    query_heads, key_heads, value_heads = split_heads(head_layout)
    length = head_layout.shape[0]
    head_count = query_heads.shape[1]
    grad_heads = grad_mixed.reshape(length, head_count, HEAD)
    block_rows = min(512, length)
    score_scale = HEAD ** (-0.5)
    grad_keys = jnp.zeros(key_heads.shape, jnp.float32)
    grad_values = jnp.zeros(value_heads.shape, jnp.float32)
    query_parts = []
    for offset in range(0, length, block_rows):
        allowed = mask_for(document_starts, offset, block_rows, length)
        query_block = query_heads[offset : offset + block_rows]
        grad_block = grad_heads[offset : offset + block_rows]
        scores = (
            jnp.einsum("qhd,khd->hqk", query_block, key_heads, preferred_element_type=jnp.float32)
            * score_scale
        )
        scores = jnp.where(allowed[None], scores, MASKED)
        probabilities = jnp.exp(scores - log_total[:, offset : offset + block_rows, None])
        grad_probs = jnp.einsum(
            "qhd,khd->hqk", grad_block, value_heads, preferred_element_type=jnp.float32
        )
        inner_sum = jnp.sum(probabilities * grad_probs, axis=-1, keepdims=True)
        grad_scores = (probabilities * (grad_probs - inner_sum)).astype(jnp.bfloat16)
        query_parts.append(
            jnp.einsum("hqk,khd->qhd", grad_scores, key_heads, preferred_element_type=jnp.float32)
            * score_scale
        )
        grad_keys = (
            grad_keys
            + jnp.einsum(
                "hqk,qhd->khd", grad_scores, query_block, preferred_element_type=jnp.float32
            )
            * score_scale
        )
        grad_values = grad_values + jnp.einsum(
            "hqk,qhd->khd",
            probabilities.astype(jnp.bfloat16),
            grad_block,
            preferred_element_type=jnp.float32,
        )
    grad_query = jnp.concatenate(query_parts, 0)
    return jnp.stack(
        [
            grad_query.reshape(length, -1),
            grad_keys.reshape(length, -1),
            grad_values.reshape(length, -1),
        ],
        axis=1,
    ).astype(jnp.bfloat16)


def on_device(
    block_input,
    seg_start,
    ln1_gain,
    ln1_bias,
    qkv_weight,
    query_bias,
    value_bias,
    query_adapter_reduce,
    query_up,
    value_adapter_reduce,
    value_up,
    out_weight,
    out_bias,
    ln2_gain,
    ln2_bias,
    fc_weight,
    fc_bias,
    proj_weight,
    proj_bias,
    grad_out,
):
    groups = block_input.shape[0]
    row_span = block_input.shape[1]
    model_width = block_input.shape[2]
    tokens = groups * row_span
    hidden_units = fc_weight.shape[1]
    row_values = block_input.reshape(tokens, model_width).astype(jnp.float32)
    normed_first, unit_first, inverse_first = norm_forward(row_values, ln1_gain, ln1_bias)
    first_hidden_layer = normed_first.astype(jnp.bfloat16)
    projected = fold_with(
        first_hidden_layer,
        jnp.zeros((tokens, 3 * model_width), jnp.float32),
        lax.all_gather(qkv_weight, "dp", axis=0, tiled=True),
    )
    query_reduce = (
        jnp.dot(first_hidden_layer, query_adapter_reduce, preferred_element_type=jnp.float32)
        * ADAPTER_SCALE
    ).astype(jnp.bfloat16)
    value_reduce = (
        jnp.dot(first_hidden_layer, value_adapter_reduce, preferred_element_type=jnp.float32)
        * ADAPTER_SCALE
    ).astype(jnp.bfloat16)
    split_parts = projected.reshape(tokens, 3, model_width)
    queries = (
        split_parts[:, 0]
        + query_bias
        + jnp.dot(query_reduce, query_up, preferred_element_type=jnp.float32)
    )
    valued = (
        split_parts[:, 2]
        + value_bias
        + jnp.dot(value_reduce, value_up, preferred_element_type=jnp.float32)
    )
    token_layout = jnp.stack([queries, split_parts[:, 1], valued], axis=1).astype(jnp.bfloat16)
    token_layout = token_layout.reshape(groups, row_span, 3, model_width)
    head_layout = lax.all_to_all(token_layout, "seq", split_axis=3, concat_axis=1, tiled=True)
    attended, log_totals = lax.map(attend_row, (head_layout, seg_start))
    mixed_tokens = jax.tree.map(
        lambda part, own: part.astype(own.dtype),
        lax.all_to_all(for_sending(attended), "seq", split_axis=1, concat_axis=2, tiled=True),
        attended,
    ).reshape(tokens, model_width)
    attention_out = fold_with(
        mixed_tokens,
        jnp.zeros((tokens, model_width), jnp.float32),
        lax.all_gather(out_weight, "dp", axis=0, tiled=True),
    )
    middle = row_values + attention_out + out_bias
    normed_second, unit_second, inverse_second = norm_forward(middle, ln2_gain, ln2_bias)
    hidden_second = normed_second.astype(jnp.bfloat16)
    before = (
        fold_with(
            hidden_second,
            jnp.zeros((tokens, hidden_units), jnp.float32),
            lax.all_gather(fc_weight, "dp", axis=0, tiled=True),
        )
        + fc_bias
    )
    gelu_value, gelu_pull = jax.vjp(partial(jax.nn.gelu, approximate=True), before)
    activated = gelu_value.astype(jnp.bfloat16)
    feed_out = fold_with(
        activated,
        jnp.zeros((tokens, model_width), jnp.float32),
        lax.all_gather(proj_weight, "dp", axis=0, tiled=True),
    )
    result_rows = middle + feed_out + proj_bias
    block_output = result_rows.astype(jnp.bfloat16).reshape(groups, row_span, model_width)
    gradient_row_list = grad_out.reshape(tokens, model_width)
    grad_act = map_with(gradient_row_list, lax.all_gather(proj_weight, "dp", axis=0, tiled=True))
    grad_before = gelu_pull(grad_act)[0].astype(jnp.bfloat16)
    grad_second = map_with(grad_before, lax.all_gather(fc_weight, "dp", axis=0, tiled=True))
    grad_middle = gradient_row_list.astype(jnp.float32) + norm_backward(
        grad_second, unit_second, inverse_second, ln2_gain
    )
    grad_attended = grad_middle.astype(jnp.bfloat16)
    grad_mixed = map_with(grad_attended, lax.all_gather(out_weight, "dp", axis=0, tiled=True))
    grad_mixed = grad_mixed.astype(jnp.bfloat16).reshape(groups, row_span, model_width)
    grad_head_layout = lax.all_to_all(grad_mixed, "seq", split_axis=2, concat_axis=1, tiled=True)
    grad_projected = lax.map(attend_back, (head_layout, grad_head_layout, log_totals, seg_start))
    grad_tokens = lax.all_to_all(
        grad_projected, "seq", split_axis=1, concat_axis=3, tiled=True
    ).reshape(tokens, 3 * model_width)
    grad_first = map_with(grad_tokens, lax.all_gather(qkv_weight, "dp", axis=0, tiled=True))
    grad_query = grad_tokens[:, :model_width]
    grad_value = grad_tokens[:, 2 * model_width :]
    gradient_query_reduce = times_transposed(grad_query, query_up).astype(jnp.bfloat16)
    gradient_value_reduce = times_transposed(grad_value, value_up).astype(jnp.bfloat16)
    grad_first = (
        grad_first
        + (
            times_transposed(gradient_query_reduce, query_adapter_reduce)
            + times_transposed(gradient_value_reduce, value_adapter_reduce)
        )
        * ADAPTER_SCALE
    )
    grad_input = grad_middle + norm_backward(grad_first, unit_first, inverse_first, ln1_gain)
    shard_query_reduce = (
        across_token_rows(first_hidden_layer, gradient_query_reduce) * ADAPTER_SCALE
    )
    local_query_up = across_token_rows(query_reduce, grad_query)
    shard_value_reduce = (
        across_token_rows(first_hidden_layer, gradient_value_reduce) * ADAPTER_SCALE
    )
    local_value_up = across_token_rows(value_reduce, grad_value)
    summed = lax.psum(
        (shard_query_reduce, local_query_up, shard_value_reduce, local_value_up), ("dp", "seq")
    )
    return (
        block_output,
        grad_input.reshape(groups, row_span, model_width),
        summed[0],
        summed[1],
        summed[2],
        summed[3],
    )


def solution(mesh):
    return jax.shard_map(
        on_device,
        mesh=mesh,
        in_specs=(
            P("dp", "seq", None),
            P("dp", None),
            P(),
            P(),
            P("dp", None),
            P(),
            P(),
            P(),
            P(),
            P(),
            P(),
            P("dp", None),
            P(),
            P(),
            P(),
            P("dp", None),
            P(),
            P("dp", None),
            P(),
            P("dp", "seq", None),
        ),
        out_specs=(P("dp", "seq", None), P("dp", "seq", None), P(), P(), P(), P()),
        check_vma=False,
    )
```

profile of v0, /device:TPU:1, one launch (start us, length us, event | category | flops | bytes accessed | tf_op | source)
XLA Modules:
  0.0 919.3 jit_solution(9611403195169453674)
XLA Ops:
  14.8 43.2 %all-gather.5.cloned.1.call-done = bf16[1024,3072]{1,0:T(8,128)(2,1)} async-done(((bf16[128,3072]{1,0:T(8,128)(2,1)}), bf16[1024,3072]{1,0:T(8,128)(2,1)}) %all-gather.5.cloned.1.call-update) | async-done | bytes 6291472 | tf_op jit(solution)/shard_map/all_gather | solution.py:195
  58.0 8.6 copy.34
  66.6 7.4 fusion.118
  78.7 3.0 copy.37
  81.6 4.1 copy.36
  85.8 3.7 fusion.56
  89.5 4.2 copy.35
  93.6 8.3 pad_maximum_fusion.1
  102.0 5.2 all-to-all-start
  107.8 137.4 %all-to-all-done = bf16[3,256,3,1024]{1,0,2,3:T(4,128)(2,1)} async-done(((bf16[3,256,3,1024]{1,0,2,3:T(4,128)(2,1)}), bf16[3,256,3,1024]{1,0,2,3:T(4,128)(2,1)}, u32[]{:S(2)}, u32[]{:S(2)}) %all-to-all-start) | async-done | bytes 4718624 | tf_op jit(solution)/shard_map/all_to_all | solution.py:218
  245.2 9.4 %copy.38 = bf16[3,4,256,3,256]{2,1,4,3,0:T(4,128)(2,1)} copy(bf16[3,4,256,3,256]{2,0,3,4,1:T(4,128)(2,1)} %bitcast.40) | data formatting | bytes 9437184 | tf_op jit(solution)/shard_map/all_to_all | solution.py:218
  254.6 8.7 all_to_all.51
  263.3 51.6 %while.22 = (s32[]{:T(128)}, bf16[3,1024,256]{1,2,0:T(8,128)(2,1)S(1)}, f32[3,4,1024]{2,1,0:T(4,128)S(1)}, bf16[3,1024,3,256]{1,3,2,0:T(8,128)(2,1)}, s32[3,1024]{1,0:T(4,128)S(1)}, /*index=5*/s32[]{:T(128)}, s32[]{:T(128)}, s32[]{}) while((s32[]{:T(128)}, bf16[3,1024,256]{1,2,0:T(8,128)(2,1)S(1)}, f32[3,4,1024]{2,1,0:T(4,128)S(1)}, ...), condition=%wide.region_7.8_spmd, body=%wide.region_2.7_spmd.sunk | while | flops 1128530432 | bytes 65192060 | solution.py:219
  267.7 2.4 fusion.241
  270.1 3.1 fusion.242
  274.9 2.4 fusion.237
  277.3 3.1 fusion.238
  284.9 2.4 fusion.241
  287.3 3.1 fusion.242
  292.1 2.4 fusion.237
  294.6 3.1 fusion.238
  302.1 2.4 fusion.241
  304.6 3.1 fusion.242
  309.4 2.4 fusion.237
  311.8 3.1 fusion.238
  316.1 2.9 copy.39
  319.1 49.9 %all_to_all.66 = bf16[3,1024,256]{2,0,1:T(4,128)(2,1)S(1)} all-to-all(bf16[3,1024,256]{2,0,1:T(4,128)(2,1)S(1)} %copy.39), channel_id=1, replica_groups=mesh['dp'=8,'seq'=4] {'seq'}, dimensions={1} | all-to-all | bytes 3145728 | tf_op jit(solution)/shard_map/all_to_all | solution.py:222
  370.9 3.6 fusion.112
  376.7 13.8 %fusion.74 = f32[768,4096]{1,0:T(8,128)} fusion(bf16[1024,4096]{1,0:T(8,128)(2,1)} %all-gather.9.cloned.1.call-done, f32[768,1024]{1,0:T(8,128)} %copy-done.6, f32[1024]{0:T(1024)S(1)} %copy-done.38, f32[1024]{0:T(1024)S(1)} %copy-done.31, f32[768]{0:T(1024)S(1)} %add_rsqrt_fusion, f32[768]{0:T(1024)S(1)} %broadcast_multiply_fusion.4), kind=kOutput, calls=%fused_computation.126 | convolution fusion | flops 6446383104 | bytes 24131584 | tf_op jit(solution)/shard_map/dot_general | solution.py:40
  390.5 27.4 %multiply_reduce_fusion.4 = (f32[768]{0:T(1024)S(1)}, f32[768]{0:T(1024)S(1)}, f32[768,1024]{1,0:T(8,128)}) fusion(f32[1024]{0:T(1024)S(1)} %copy-done.31, f32[768]{0:T(1024)S(1)} %add_rsqrt_fusion, f32[768,1024]{1,0:T(8,128)S(1)} %copy-done.7, f32[768]{0:T(1024)S(1)} %broadcast_multiply_fusion.4, bf16[1024,4096]{1,0:T(8,128)(2,1)} %all-gather.9.cloned.1.call-done, ...), kind=kOutput, calls=%fused_computation.124 | convolution fusion | flops 12955678720 | bytes 37257216 | tf_op jit(solution)/shard_map/dot_general | solution.py:44
  418.0 3.1 multiply_add_fusion
  422.9 2.6 copy.41
  425.5 3.6 all-to-all-start.2
  429.2 47.6 %all-to-all-done.2 = bf16[3,256,1024]{1,0,2:T(4,128)(2,1)S(1)} async-done(((bf16[3,256,1024]{1,0,2:T(4,128)(2,1)}), bf16[3,256,1024]{1,0,2:T(4,128)(2,1)S(1)}, u32[]{:S(2)}, u32[]{:S(2)}) %all-to-all-start.2) | async-done | bytes 1572896 | tf_op jit(solution)/shard_map/all_to_all | solution.py:260
  476.8 2.6 copy.42
  479.4 2.8 all_to_all.58
  482.3 106.2 %while.23 = (s32[]{:T(128)}, bf16[3,1024,3,256]{1,3,2,0:T(8,128)(2,1)}, bf16[3,1024,3,256]{1,3,2,0:T(8,128)(2,1)}, s32[3,1024]{1,0:T(4,128)S(1)}, f32[3,4,1024]{...) while((s32[]{:T(128)}, bf16[3,1024,3,256]{1,3,2,0:T(8,128)(2,1)}, ...), condition=%wide.region_15.16_spmd, body=%wide.region_12.15_spmd.sunk | while | flops 2758013440 | bytes 152731792 | solution.py:261
  487.7 2.4 fusion.269
  490.1 2.5 fusion.272
  492.6 5.4 multiply_reduce_fusion.8
  498.0 5.5 multiply_reduce_fusion.7
  503.5 8.3 multiply_convert_fusion.7
  523.0 2.4 fusion.269
  525.4 2.5 fusion.272
  527.9 5.4 multiply_reduce_fusion.8
  533.3 5.5 multiply_reduce_fusion.7
  538.8 8.3 multiply_convert_fusion.7
  558.3 2.4 fusion.269
  560.7 2.5 fusion.272
  563.2 5.4 multiply_reduce_fusion.8
  568.6 5.5 multiply_reduce_fusion.7
  574.1 8.3 multiply_convert_fusion.7
  588.5 10.3 %copy.43 = bf16[3,1024,3,256]{3,2,0,1:T(4,128)(2,1)} copy(bf16[3,1024,3,256]{1,3,2,0:T(8,128)(2,1)} %get-tuple-element.68) | data formatting | bytes 9437184 | tf_op jit(solution)/shard_map/while | solution.py:261
  598.8 5.5 all-to-all-start.3
  604.4 14.5 %add_convert_fusion = bf16[768,1024]{1,0:T(8,128)(2,1)} fusion(f32[768,1024]{1,0:T(8,128)S(1)} %copy-done.8, bf16[4096,1024]{1,0:T(8,128)(2,1)} %all-gather.11.cloned.1.call-done, f32[768,4096]{1,0:T(8,128)} %fusion.74, f32[4096]{0:T(1024)S(1)} %copy-done.36, f32[1024]{0:T(1024)S(1)} %copy-done.39), kind=kOutput, calls=%fused_computation.120 | convolution fusion | flops 6476267520 | bytes 25710592 | tf_op jit(solution)/shard_map/dot_general | solution.py:40
  618.8 123.1 %all-to-all-done.3 = bf16[3,1024,3,256]{3,2,0,1:T(4,128)(2,1)} async-done(((bf16[3,1024,3,256]{3,2,0,1:T(4,128)(2,1)}), bf16[3,1024,3,256]{3,2,0,1:T(4,128)(2,1)}, u32[]{:S(2)}, u32[]{:S(2)}) %all-to-all-start.3) | async-done | bytes 4718624 | tf_op jit(solution)/shard_map/all_to_all | solution.py:262
  741.9 11.0 %copy.47 = bf16[3,4,256,3,256]{4,1,3,2,0:T(4,128)(2,1)} copy(bf16[3,4,256,3,256]{4,3,0,2,1:T(4,128)(2,1)} %bitcast.48) | data formatting | bytes 9437184 | tf_op jit(solution)/shard_map/all_to_all | solution.py:262
  753.0 9.6 %reshape.412 = bf16[768,3072]{1,0:T(8,128)(2,1)} reshape(bf16[3,256,3,4,256]{4,3,2,1,0:T(4,128)(2,1)} %bitcast.288) | data formatting | bytes 9437184 | tf_op jit(solution)/shard_map/reshape | solution.py:264
  766.5 2.4 fusion.84
  768.9 2.3 fusion.80
  775.4 8.7 fusion.119
  784.2 2.9 fusion.106
  787.1 5.4 fusion.72
  792.5 114.5 %all-reduce.3.cloned.1.call-done = (f32[1024,4]{0,1:T(4,128)}, f32[4,1024]{1,0:T(4,128)}, f32[1024,4]{0,1:T(4,128)}, f32[4,1024]{1,0:T(4,128)}) async-done(((f32[1024,4]{0,1:T(4,128)}, f32[4,1024]{1,0:T(4,128)}, f32[1024,4]{0,1:T(4,128)}, f32[4,1024]{1,0:T(4,128)}), (f32[1024,4]{0,1:T(4,128)}, f32[4,1024]{1,0:T(4,128)}, f32[1024,4]{0,1:T(4,128)}, f32[4,1024]{1,0:T(4,128)})) %all-reduce.3.cloned.1.call-update) | async-done | bytes 65552 | tf_op jit(solution)/shard_map/psum | solution.py:287
  (216 shorter events, 84.6 us)
Async XLA Ops:
  7.2 5.3 copy-start
  7.2 4.0 copy-start.1
  7.2 4.6 copy-start.22
  7.2 4.6 copy-start.26
  7.2 50.8 %all-gather.5.cloned.1.call-start = ((), (), s32[]{:S(2)}) async-start(), calls=%async_computation.4 | async-start | bytes 7077888 | tf_op jit(solution)/shard_map/all_gather | solution.py:195
  7.9 362.9 %all-gather.7.cloned.1.call-start = ((), (), s32[]{:S(2)}) async-start(), calls=%async_computation.5 | async-start | bytes 2359296 | tf_op jit(solution)/shard_map/all_gather | solution.py:228
  8.7 368.0 %all-gather.9.cloned.1.call-start = ((), (), s32[]{:S(2)}) async-start(), calls=%async_computation.6 | async-start | bytes 9437184 | tf_op jit(solution)/shard_map/all_gather | solution.py:237
  9.4 4.2 copy-start.24
  11.2 1.8 copy-start.14
  11.8 1.2 copy-start.16
  12.4 1.2 copy-start.4
  13.6 62.0 %copy-start.18 = (bf16[768,4]{0,1:T(4,128)(2,1)}, bf16[768,4]{0,1:T(4,128)(2,1)S(1)}, u32[]{:S(2)}) copy-start(bf16[768,4]{0,1:T(4,128)(2,1)S(1)} %fusion.89) | copy-start | bytes 18436
  14.1 71.6 %copy-start.20 = (bf16[768,4]{0,1:T(4,128)(2,1)}, bf16[768,4]{0,1:T(4,128)(2,1)S(1)}, u32[]{:S(2)}) copy-start(bf16[768,4]{0,1:T(4,128)(2,1)S(1)} %fusion.88) | copy-start | bytes 18436
  66.6 9.0 copy-start.27
  66.6 9.0 copy-start.32
  74.0 4.6 copy-start.11
  78.7 7.1 copy-start.29
  78.7 7.1 copy-start.33
  102.0 143.3 %all-to-all-start = ((bf16[3,256,3,1024]{1,0,2,3:T(4,128)(2,1)}), bf16[3,256,3,1024]{1,0,2,3:T(4,128)(2,1)}, u32[]{:S(2)}, u32[]{:S(2)}) async-start(bf16[3,256,3,1024]{1,0,2,3:T(4,128)(2,1)} %pad_maximum_fusion.1), calls=%async_computation | async-start | bytes 12582912 | tf_op jit(solution)/shard_map/all_to_all | solution.py:218
  107.2 283.3 %all-gather.11.cloned.1.call-start = ((), (), s32[]{:S(2)}) async-start(), calls=%async_computation.7 | async-start | bytes 9437184 | tf_op jit(solution)/shard_map/all_gather | solution.py:246
  254.6 8.7 copy-start.13
  315.0 1.1 copy-start.12
  369.0 1.9 copy-start.2
  369.0 1.9 copy-start.37
  370.9 5.8 copy-start.31
  370.9 5.8 copy-start.38
  374.5 1.7 copy-start.6
  376.6 13.9 %copy-start.7 = (f32[768,1024]{1,0:T(8,128)S(1)}, f32[768,1024]{1,0:T(8,128)}, u32[]{:S(2)}) copy-start(f32[768,1024]{1,0:T(8,128)} %copy-done.6) | copy-start | bytes 9437188
  376.6 13.9 %copy-start.35 = (f32[4096]{0:T(1024)S(1)}, f32[4096]{0:T(1024)}, u32[]{:S(2)}) copy-start(f32[4096]{0:T(1024)} %param.40) | copy-start | bytes 49156
  418.0 3.1 copy-start.34
  421.1 1.8 copy-start.9
  425.5 51.3 %all-to-all-start.2 = ((bf16[3,256,1024]{1,0,2:T(4,128)(2,1)}), bf16[3,256,1024]{1,0,2:T(4,128)(2,1)S(1)}, u32[]{:S(2)}, u32[]{:S(2)}) async-start(bf16[3,256,1024]{1,0,2:T(4,128)(2,1)} %copy.41), calls=%async_computation.2 | async-start | bytes 4194304 | tf_op jit(solution)/shard_map/all_to_all | solution.py:260
  598.8 5.6 copy-start.8
  598.8 5.6 copy-start.36
  598.8 5.6 copy-start.39
  598.8 143.1 %all-to-all-start.3 = ((bf16[3,1024,3,256]{3,2,0,1:T(4,128)(2,1)}), bf16[3,1024,3,256]{3,2,0,1:T(4,128)(2,1)}, u32[]{:S(2)}, u32[]{:S(2)}) async-start(bf16[3,1024,3,256]{3,2,0,1:T(4,128)(2,1)} %copy.43), calls=%async_computation.3 | async-start | bytes 12582912 | tf_op jit(solution)/shard_map/all_to_all | solution.py:262
  604.3 302.7 %all-reduce.3.cloned.1.call-start = ((), (), s32[]{:S(2)}) async-start(), calls=%async_computation.8 | async-start | bytes 131072 | tf_op jit(solution)/shard_map/psum | solution.py:287
  753.0 9.6 %copy-start.28 = (bf16[4,1024]{1,0:T(4,128)(2,1)S(1)}, bf16[4,1024]{1,0:T(4,128)(2,1)}, u32[]{:S(2)}) copy-start(bf16[4,1024]{1,0:T(4,128)(2,1)} %param.34) | copy-start | bytes 24580
  753.0 11.7 %copy-start.30 = (bf16[4,1024]{1,0:T(4,128)(2,1)S(1)}, bf16[4,1024]{1,0:T(4,128)(2,1)}, u32[]{:S(2)}) copy-start(bf16[4,1024]{1,0:T(4,128)(2,1)} %param.32) | copy-start | bytes 24580
  753.0 13.6 %copy-start.21 = (bf16[768,4]{0,1:T(4,128)(2,1)S(1)}, bf16[768,4]{0,1:T(4,128)(2,1)}, u32[]{:S(2)}) copy-start(bf16[768,4]{0,1:T(4,128)(2,1)} %copy-done.20) | copy-start | bytes 18436
  762.5 6.4 copy-start.19
  762.6 8.7 copy-start.5
  762.6 9.6 %copy-start.25 = (bf16[1024,4]{0,1:T(4,128)(2,1)S(1)}, bf16[1024,4]{0,1:T(4,128)(2,1)}, u32[]{:S(2)}) copy-start(bf16[1024,4]{0,1:T(4,128)(2,1)} %param.31) | copy-start | bytes 24580
  775.4 8.8 copy-start.3
  775.4 8.8 copy-start.10
  775.4 8.8 copy-start.15
  775.4 8.8 copy-start.17
  775.4 8.8 copy-start.23
Sparse Core Ops, SparseCore 0:
  9.9 48.0 all-gather.4
  59.9 27.8 all-gather.6
  89.7 54.3 all-gather.8
  145.9 54.3 all-gather.10
  787.2 119.7 all-reduce.2
where the time goes:
time: 928 us; the launch traced here: 919 us
  waiting for transfers between devices  468 us (50%)
  matrix products  197 us (21%)
  local copies, waits for them, and re-layouts  103 us (11%)
  other arithmetic  70.1 us (8%)
  blocking collectives  49.9 us (5%)
  between operations  14.8 us (2%)
  starting transfers between devices  14.7 us (2%)
    all_to_all x1, waiting for transfers between devices, on_device(): lax.all_to_all(token_layout, 'seq', split_axis=3, concat_axis=1, tiled=True)  137 us
    all_to_all x1, waiting for transfers between devices, on_device(): lax.all_to_all(grad_projected, 'seq', split_axis=1, concat_axis=3, tiled=...  123 us
    psum x1, waiting for transfers between devices, on_device(): lax.psum((shard_query_reduce, local_query_up, shard_value_reduce, local_v...  114 us
    all_to_all x1, blocking collectives, on_device(): lax.all_to_all(for_sending(attended), 'seq', split_axis=1, concat_axis=2,...  49.9 us
    all_to_all x1, waiting for transfers between devices, on_device(): lax.all_to_all(grad_mixed, 'seq', split_axis=2, concat_axis=1, tiled=True)  47.6 us
    dot_general x7, matrix products, times_transposed(): lax.dot_general(left_side, right_side, (((1,), (1,)), ((), ())), preferre...  47.1 us
    all_gather x1, waiting for transfers between devices, on_device(): lax.all_gather(qkv_weight, 'dp', axis=0, tiled=True)  43.2 us
    dot_general x4, matrix products, fold_with(): jnp.dot(columns, weight_piece, preferred_element_type=jnp.float32)  39.2 us
  transfers between devices with their start and end apart: 8, of which 5 were waited for; matrix products, arithmetic and copies ran while one was open for 16% of the time, Pallas kernels for 0%

commit v1 on v0

--- a/solution.py
+++ b/solution.py
@@ -285,7 +285,8 @@
     )
     local_value_up = across_token_rows(value_reduce, grad_value)
     summed = lax.psum(
-        (shard_query_reduce, local_query_up, shard_value_reduce, local_value_up), ("dp", "seq")
+        lax.psum((shard_query_reduce, local_query_up, shard_value_reduce, local_value_up), "seq"),
+        "dp",
     )
     return (
         block_output,

time: 928 us -> 899 us (0.969)
  waiting for transfers between devices: 468 us -> 437 us
    psum x1, waiting for transfers between devices: 114 us -> 31.1 us  [on_device(): lax.psum((shard_query_reduce, local_query_up, shard_value_reduce, local_v...]
    psum x0 -> x1, waiting for transfers between devices: none -> 52.3 us  [on_device(): lax.psum(lax.psum((shard_query_reduce, local_query_up, shard_value_reduce...]
  transfers between devices with their start and end apart: 8 -> 9, of which waited for: 5 -> 6; matrix products, arithmetic and copies ran while one was open for 16% -> 17% of each run, Pallas kernels for 0% -> 0%
where the time goes in v1:
time: 899 us; the launch traced here: 889 us
  waiting for transfers between devices  437 us (49%)
  matrix products  197 us (22%)
  local copies, waits for them, and re-layouts  103 us (11%)
  other arithmetic  70.1 us (8%)
  blocking collectives  49.9 us (6%)
  between operations  15.1 us (2%)
  starting transfers between devices  14.8 us (2%)
    all_to_all x1, waiting for transfers between devices, on_device(): lax.all_to_all(token_layout, 'seq', split_axis=3, concat_axis=1, tiled=True)  137 us
    all_to_all x1, waiting for transfers between devices, on_device(): lax.all_to_all(grad_projected, 'seq', split_axis=1, concat_axis=3, tiled=...  123 us
    psum x1, waiting for transfers between devices, on_device(): lax.psum(lax.psum((shard_query_reduce, local_query_up, shard_value_reduce...  52.3 us
    all_to_all x1, blocking collectives, on_device(): lax.all_to_all(for_sending(attended), 'seq', split_axis=1, concat_axis=2,...  49.9 us
    all_to_all x1, waiting for transfers between devices, on_device(): lax.all_to_all(grad_mixed, 'seq', split_axis=2, concat_axis=1, tiled=True)  47.6 us
    dot_general x7, matrix products, times_transposed(): lax.dot_general(left_side, right_side, (((1,), (1,)), ((), ())), preferre...  47.2 us
    all_gather x1, waiting for transfers between devices, on_device(): lax.all_gather(qkv_weight, 'dp', axis=0, tiled=True)  43.2 us
    dot_general x4, matrix products, fold_with(): jnp.dot(columns, weight_piece, preferred_element_type=jnp.float32)  39.2 us
  transfers between devices with their start and end apart: 9, of which 6 were waited for; matrix products, arithmetic and copies ran while one was open for 17% of the time, Pallas kernels for 0%

profile of v1, /device:TPU:1, one launch (start us, length us, event | category | flops | bytes accessed | tf_op | source)
XLA Modules:
  0.0 888.7 jit_solution(8683328753034579786)
XLA Ops:
  14.8 43.2 %all-gather.5.cloned.1.call-done = bf16[1024,3072]{1,0:T(8,128)(2,1)} async-done(((bf16[128,3072]{1,0:T(8,128)(2,1)}), bf16[1024,3072]{1,0:T(8,128)(2,1)}) %all-gather.5.cloned.1.call-update) | async-done | bytes 6291472 | tf_op jit(solution)/shard_map/all_gather | solution.py:195
  58.0 8.7 copy.34
  66.7 7.4 fusion.118
  78.7 3.0 copy.37
  81.6 4.1 copy.36
  85.8 3.7 fusion.56
  89.5 4.2 copy.35
  93.6 8.3 pad_maximum_fusion.1
  102.0 5.2 all-to-all-start
  107.8 137.4 %all-to-all-done = bf16[3,256,3,1024]{1,0,2,3:T(4,128)(2,1)} async-done(((bf16[3,256,3,1024]{1,0,2,3:T(4,128)(2,1)}), bf16[3,256,3,1024]{1,0,2,3:T(4,128)(2,1)}, u32[]{:S(2)}, u32[]{:S(2)}) %all-to-all-start) | async-done | bytes 4718624 | tf_op jit(solution)/shard_map/all_to_all | solution.py:218
  245.2 9.4 %copy.38 = bf16[3,4,256,3,256]{2,1,4,3,0:T(4,128)(2,1)} copy(bf16[3,4,256,3,256]{2,0,3,4,1:T(4,128)(2,1)} %bitcast.40) | data formatting | bytes 9437184 | tf_op jit(solution)/shard_map/all_to_all | solution.py:218
  254.6 8.7 all_to_all.51
  263.4 51.6 %while.22 = (s32[]{:T(128)}, bf16[3,1024,256]{1,2,0:T(8,128)(2,1)S(1)}, f32[3,4,1024]{2,1,0:T(4,128)S(1)}, bf16[3,1024,3,256]{1,3,2,0:T(8,128)(2,1)}, s32[3,1024]{1,0:T(4,128)S(1)}, /*index=5*/s32[]{:T(128)}, s32[]{:T(128)}, s32[]{}) while((s32[]{:T(128)}, bf16[3,1024,256]{1,2,0:T(8,128)(2,1)S(1)}, f32[3,4,1024]{2,1,0:T(4,128)S(1)}, ...), condition=%wide.region_7.8_spmd, body=%wide.region_2.7_spmd.sunk | while | flops 1128530432 | bytes 65192060 | solution.py:219
  267.7 2.4 fusion.241
  270.1 3.1 fusion.242
  274.9 2.4 fusion.237
  277.3 3.1 fusion.238
  284.9 2.4 fusion.241
  287.3 3.1 fusion.242
  292.1 2.4 fusion.237
  294.6 3.1 fusion.238
  302.1 2.4 fusion.241
  304.6 3.1 fusion.242
  309.4 2.4 fusion.237
  311.8 3.1 fusion.238
  316.2 2.9 copy.39
  319.1 49.9 %all_to_all.66 = bf16[3,1024,256]{2,0,1:T(4,128)(2,1)S(1)} all-to-all(bf16[3,1024,256]{2,0,1:T(4,128)(2,1)S(1)} %copy.39), channel_id=1, replica_groups=mesh['dp'=8,'seq'=4] {'seq'}, dimensions={1} | all-to-all | bytes 3145728 | tf_op jit(solution)/shard_map/all_to_all | solution.py:222
  370.9 3.6 fusion.112
  376.7 13.8 %fusion.74 = f32[768,4096]{1,0:T(8,128)} fusion(bf16[1024,4096]{1,0:T(8,128)(2,1)} %all-gather.9.cloned.1.call-done, f32[768,1024]{1,0:T(8,128)} %copy-done.6, f32[1024]{0:T(1024)S(1)} %copy-done.38, f32[1024]{0:T(1024)S(1)} %copy-done.31, f32[768]{0:T(1024)S(1)} %add_rsqrt_fusion, f32[768]{0:T(1024)S(1)} %broadcast_multiply_fusion.4), kind=kOutput, calls=%fused_computation.126 | convolution fusion | flops 6446383104 | bytes 24131584 | tf_op jit(solution)/shard_map/dot_general | solution.py:40
  390.6 27.5 %multiply_reduce_fusion.4 = (f32[768]{0:T(1024)S(1)}, f32[768]{0:T(1024)S(1)}, f32[768,1024]{1,0:T(8,128)}) fusion(f32[1024]{0:T(1024)S(1)} %copy-done.31, f32[768]{0:T(1024)S(1)} %add_rsqrt_fusion, f32[768,1024]{1,0:T(8,128)S(1)} %copy-done.7, f32[768]{0:T(1024)S(1)} %broadcast_multiply_fusion.4, bf16[1024,4096]{1,0:T(8,128)(2,1)} %all-gather.9.cloned.1.call-done, ...), kind=kOutput, calls=%fused_computation.124 | convolution fusion | flops 12955678720 | bytes 37257216 | tf_op jit(solution)/shard_map/dot_general | solution.py:44
  418.0 3.1 multiply_add_fusion
  423.0 2.6 copy.41
  425.6 3.6 all-to-all-start.2
  429.2 47.6 %all-to-all-done.2 = bf16[3,256,1024]{1,0,2:T(4,128)(2,1)S(1)} async-done(((bf16[3,256,1024]{1,0,2:T(4,128)(2,1)}), bf16[3,256,1024]{1,0,2:T(4,128)(2,1)S(1)}, u32[]{:S(2)}, u32[]{:S(2)}) %all-to-all-start.2) | async-done | bytes 1572896 | tf_op jit(solution)/shard_map/all_to_all | solution.py:260
  476.9 2.6 copy.42
  479.5 2.8 all_to_all.58
  482.3 106.3 %while.23 = (s32[]{:T(128)}, bf16[3,1024,3,256]{1,3,2,0:T(8,128)(2,1)}, bf16[3,1024,3,256]{1,3,2,0:T(8,128)(2,1)}, s32[3,1024]{1,0:T(4,128)S(1)}, f32[3,4,1024]{...) while((s32[]{:T(128)}, bf16[3,1024,3,256]{1,3,2,0:T(8,128)(2,1)}, ...), condition=%wide.region_15.16_spmd, body=%wide.region_12.15_spmd.sunk | while | flops 2758013440 | bytes 152731792 | solution.py:261
  487.8 2.4 fusion.269
  490.2 2.5 fusion.272
  492.7 5.4 multiply_reduce_fusion.8
  498.1 5.5 multiply_reduce_fusion.7
  503.6 8.3 multiply_convert_fusion.7
  523.1 2.4 fusion.269
  525.6 2.5 fusion.272
  528.0 5.4 multiply_reduce_fusion.8
  533.4 5.5 multiply_reduce_fusion.7
  538.9 8.3 multiply_convert_fusion.7
  558.4 2.4 fusion.269
  560.9 2.5 fusion.272
  563.4 5.4 multiply_reduce_fusion.8
  568.8 5.5 multiply_reduce_fusion.7
  574.3 8.3 multiply_convert_fusion.7
  588.6 10.2 %copy.43 = bf16[3,1024,3,256]{3,2,0,1:T(4,128)(2,1)} copy(bf16[3,1024,3,256]{1,3,2,0:T(8,128)(2,1)} %get-tuple-element.68) | data formatting | bytes 9437184 | tf_op jit(solution)/shard_map/while | solution.py:261
  598.9 5.5 all-to-all-start.3
  604.5 14.5 %add_convert_fusion = bf16[768,1024]{1,0:T(8,128)(2,1)} fusion(f32[768,1024]{1,0:T(8,128)S(1)} %copy-done.8, bf16[4096,1024]{1,0:T(8,128)(2,1)} %all-gather.11.cloned.1.call-done, f32[768,4096]{1,0:T(8,128)} %fusion.74, f32[4096]{0:T(1024)S(1)} %copy-done.36, f32[1024]{0:T(1024)S(1)} %copy-done.39), kind=kOutput, calls=%fused_computation.120 | convolution fusion | flops 6476267520 | bytes 25710592 | tf_op jit(solution)/shard_map/dot_general | solution.py:40
  618.9 123.1 %all-to-all-done.3 = bf16[3,1024,3,256]{3,2,0,1:T(4,128)(2,1)} async-done(((bf16[3,1024,3,256]{3,2,0,1:T(4,128)(2,1)}), bf16[3,1024,3,256]{3,2,0,1:T(4,128)(2,1)}, u32[]{:S(2)}, u32[]{:S(2)}) %all-to-all-start.3) | async-done | bytes 4718624 | tf_op jit(solution)/shard_map/all_to_all | solution.py:262
  742.0 11.1 %copy.47 = bf16[3,4,256,3,256]{4,1,3,2,0:T(4,128)(2,1)} copy(bf16[3,4,256,3,256]{4,3,0,2,1:T(4,128)(2,1)} %bitcast.48) | data formatting | bytes 9437184 | tf_op jit(solution)/shard_map/all_to_all | solution.py:262
  753.1 9.6 %reshape.412 = bf16[768,3072]{1,0:T(8,128)(2,1)} reshape(bf16[3,256,3,4,256]{4,3,2,1,0:T(4,128)(2,1)} %bitcast.288) | data formatting | bytes 9437184 | tf_op jit(solution)/shard_map/reshape | solution.py:264
  766.6 2.4 fusion.84
  775.5 8.7 fusion.119
  784.3 2.9 fusion.106
  787.3 31.1 %all-reduce.7.cloned.1.call-done = (f32[1024,4]{0,1:T(4,128)}, f32[4,1024]{1,0:T(4,128)}, f32[1024,4]{0,1:T(4,128)}, f32[4,1024]{1,0:T(4,128)}) async-done(((f32[1024,4]{0,1:T(4,128)}, f32[4,1024]{1,0:T(4,128)}, f32[1024,4]{0,1:T(4,128)}, f32[4,1024]{1,0:T(4,128)}), (f32[1024,4]{0,1:T(4,128)}, f32[4,1024]{1,0:T(4,128)}, f32[1024,4]{0,1:T(4,128)}, f32[4,1024]{1,0:T(4,128)})) %all-reduce.7.cloned.1.call-update) | async-done | bytes 65552 | tf_op jit(solution)/shard_map/psum | solution.py:288
  818.4 5.4 fusion.72
  823.9 52.3 %all-reduce.5.cloned.1.call-done = (f32[1024,4]{0,1:T(4,128)}, f32[4,1024]{1,0:T(4,128)}, f32[1024,4]{0,1:T(4,128)}, f32[4,1024]{1,0:T(4,128)}) async-done(((f32[1024,4]{0,1:T(4,128)}, f32[4,1024]{1,0:T(4,128)}, f32[1024,4]{0,1:T(4,128)}, f32[4,1024]{1,0:T(4,128)}), (f32[1024,4]{0,1:T(4,128)}, f32[4,1024]{1,0:T(4,128)}, f32[1024,4]{0,1:T(4,128)}, f32[4,1024]{1,0:T(4,128)})) %all-reduce.5.cloned.1.call-update) | async-done | bytes 65552 | tf_op jit(solution)/shard_map/psum | solution.py:287
  (219 shorter events, 87.0 us)
Async XLA Ops:
  7.2 5.3 copy-start
  7.2 4.0 copy-start.1
  7.2 4.6 copy-start.22
  7.2 4.6 copy-start.26
  7.2 50.8 %all-gather.5.cloned.1.call-start = ((), (), s32[]{:S(2)}) async-start(), calls=%async_computation.4 | async-start | bytes 7077888 | tf_op jit(solution)/shard_map/all_gather | solution.py:195
  7.9 362.9 %all-gather.7.cloned.1.call-start = ((), (), s32[]{:S(2)}) async-start(), calls=%async_computation.5 | async-start | bytes 2359296 | tf_op jit(solution)/shard_map/all_gather | solution.py:228
  8.7 368.0 %all-gather.9.cloned.1.call-start = ((), (), s32[]{:S(2)}) async-start(), calls=%async_computation.6 | async-start | bytes 9437184 | tf_op jit(solution)/shard_map/all_gather | solution.py:237
  9.4 4.2 copy-start.24
  11.2 1.8 copy-start.14
  11.8 1.2 copy-start.16
  12.4 1.2 copy-start.4
  13.6 62.1 %copy-start.18 = (bf16[768,4]{0,1:T(4,128)(2,1)}, bf16[768,4]{0,1:T(4,128)(2,1)S(1)}, u32[]{:S(2)}) copy-start(bf16[768,4]{0,1:T(4,128)(2,1)S(1)} %fusion.89) | copy-start | bytes 18436
  14.1 71.7 %copy-start.20 = (bf16[768,4]{0,1:T(4,128)(2,1)}, bf16[768,4]{0,1:T(4,128)(2,1)S(1)}, u32[]{:S(2)}) copy-start(bf16[768,4]{0,1:T(4,128)(2,1)S(1)} %fusion.88) | copy-start | bytes 18436
  66.7 9.0 %copy-start.27 = (bf16[4,1024]{1,0:T(4,128)(2,1)S(1)}, bf16[4,1024]{1,0:T(4,128)(2,1)}, u32[]{:S(2)}) copy-start(bf16[4,1024]{1,0:T(4,128)(2,1)} %param.34) | copy-start | bytes 24580
  66.7 9.0 %copy-start.32 = (f32[1024]{0:T(1024)S(1)}, f32[1024]{0:T(1024)}, u32[]{:S(2)}) copy-start(f32[1024]{0:T(1024)} %param.30) | copy-start | bytes 12292
  74.0 4.6 copy-start.11
  78.7 7.1 copy-start.29
  78.7 7.1 copy-start.33
  102.0 143.3 %all-to-all-start = ((bf16[3,256,3,1024]{1,0,2,3:T(4,128)(2,1)}), bf16[3,256,3,1024]{1,0,2,3:T(4,128)(2,1)}, u32[]{:S(2)}, u32[]{:S(2)}) async-start(bf16[3,256,3,1024]{1,0,2,3:T(4,128)(2,1)} %pad_maximum_fusion.1), calls=%async_computation | async-start | bytes 12582912 | tf_op jit(solution)/shard_map/all_to_all | solution.py:218
  107.2 283.3 %all-gather.11.cloned.1.call-start = ((), (), s32[]{:S(2)}) async-start(), calls=%async_computation.7 | async-start | bytes 9437184 | tf_op jit(solution)/shard_map/all_gather | solution.py:246
  254.6 8.7 copy-start.13
  315.0 1.1 copy-start.12
  369.0 1.9 copy-start.2
  369.0 1.9 copy-start.37
  370.9 5.8 copy-start.31
  370.9 5.8 copy-start.38
  374.5 1.7 copy-start.6
  376.6 13.9 %copy-start.7 = (f32[768,1024]{1,0:T(8,128)S(1)}, f32[768,1024]{1,0:T(8,128)}, u32[]{:S(2)}) copy-start(f32[768,1024]{1,0:T(8,128)} %copy-done.6) | copy-start | bytes 9437188
  376.6 13.9 %copy-start.35 = (f32[4096]{0:T(1024)S(1)}, f32[4096]{0:T(1024)}, u32[]{:S(2)}) copy-start(f32[4096]{0:T(1024)} %param.40) | copy-start | bytes 49156
  418.0 3.1 copy-start.34
  421.2 1.8 copy-start.9
  425.6 51.3 %all-to-all-start.2 = ((bf16[3,256,1024]{1,0,2:T(4,128)(2,1)}), bf16[3,256,1024]{1,0,2:T(4,128)(2,1)S(1)}, u32[]{:S(2)}, u32[]{:S(2)}) async-start(bf16[3,256,1024]{1,0,2:T(4,128)(2,1)} %copy.41), calls=%async_computation.2 | async-start | bytes 4194304 | tf_op jit(solution)/shard_map/all_to_all | solution.py:260
  598.9 5.6 copy-start.8
  598.9 5.6 copy-start.36
  598.9 5.6 copy-start.39
  598.9 143.2 %all-to-all-start.3 = ((bf16[3,1024,3,256]{3,2,0,1:T(4,128)(2,1)}), bf16[3,1024,3,256]{3,2,0,1:T(4,128)(2,1)}, u32[]{:S(2)}, u32[]{:S(2)}) async-start(bf16[3,1024,3,256]{3,2,0,1:T(4,128)(2,1)} %copy.43), calls=%async_computation.3 | async-start | bytes 12582912 | tf_op jit(solution)/shard_map/all_to_all | solution.py:262
  604.4 214.0 %all-reduce.7.cloned.1.call-start = ((), (), s32[]{:S(2)}) async-start(), calls=%async_computation.9 | async-start | bytes 131072 | tf_op jit(solution)/shard_map/psum | solution.py:288
  753.1 9.6 %copy-start.28 = (bf16[4,1024]{1,0:T(4,128)(2,1)S(1)}, bf16[4,1024]{1,0:T(4,128)(2,1)}, u32[]{:S(2)}) copy-start(bf16[4,1024]{1,0:T(4,128)(2,1)} %param.34) | copy-start | bytes 24580
  753.1 11.6 %copy-start.30 = (bf16[4,1024]{1,0:T(4,128)(2,1)S(1)}, bf16[4,1024]{1,0:T(4,128)(2,1)}, u32[]{:S(2)}) copy-start(bf16[4,1024]{1,0:T(4,128)(2,1)} %param.32) | copy-start | bytes 24580
  753.1 13.6 %copy-start.21 = (bf16[768,4]{0,1:T(4,128)(2,1)S(1)}, bf16[768,4]{0,1:T(4,128)(2,1)}, u32[]{:S(2)}) copy-start(bf16[768,4]{0,1:T(4,128)(2,1)} %copy-done.20) | copy-start | bytes 18436
  762.7 6.4 copy-start.19
  762.7 8.7 copy-start.5
  762.7 9.6 %copy-start.25 = (bf16[1024,4]{0,1:T(4,128)(2,1)S(1)}, bf16[1024,4]{0,1:T(4,128)(2,1)}, u32[]{:S(2)}) copy-start(bf16[1024,4]{0,1:T(4,128)(2,1)} %param.31) | copy-start | bytes 24580
  775.5 8.8 copy-start.3
  775.5 8.8 copy-start.10
  775.5 8.8 copy-start.15
  775.5 8.8 copy-start.17
  775.5 8.8 copy-start.23
  787.2 88.9 %all-reduce.5.cloned.1.call-start = ((), (), s32[]{:S(2)}) async-start(), calls=%async_computation.8 | async-start | bytes 131072 | tf_op jit(solution)/shard_map/psum | solution.py:287
Sparse Core Ops, SparseCore 0:
  9.9 48.0 all-gather.4
  59.9 27.8 all-gather.6
  89.7 54.3 all-gather.8
  145.9 54.3 all-gather.10
  787.3 31.0 all-reduce.6
  821.9 54.1 all-reduce.4
